TPU v7x, 128 devices: a whole 4x4x4 slice. The times are simulated.
128 devices in a mesh: section: 2 (over z_hi), ep: 32 (over x, y, core), dp: 2 (over z_lo).
Axes of the slice: x: 4, y: 4, z: 4 (z_hi: 2, z_lo: 2; z = z_hi * 2 + z_lo), core: 2. Of those that a mesh axis runs over, the one named last changes fastest.
Arguments:
- samples: float32 [4, 128, 64, 160], P(('section', 'dp'), None, 'ep'), may hold values from -0.3 to 0.3
- req_frames: int32 [4, 32, 4], P(('section', 'dp'), 'ep'), may hold values from 1 to 64, 128 in all within a row
- w_in: bfloat16 [128, 1280], replicated, may hold values from -0.5 to 0.5
- w_up_aud: bfloat16 [1280, 2560], P(None, 'dp'), may hold values from -0.15625 to 0.15625
- w_down_aud: bfloat16 [2560, 1280], P('dp'), may hold values from -0.125 to 0.125
- w_out: bfloat16 [1280, 2048], replicated, may hold values from -0.15625 to 0.15625
- norm_gain: float32 [2048], replicated, may hold values from 0.1 to 1.9
- expert_ids: int32 [4, 4096, 8], P(('section', 'dp'), 'ep'), may hold values from 0 to 63, all different within a row; in each aligned block of 128 rows (0 to 127, 128 to 255, ..., all dimensions but the last counted through in order) at most 20 rows name the same one
- gate_weights: float32 [4, 4096, 8], P(('section', 'dp'), 'ep'), may hold values from 0.03 to 0.3
- cotangent: bfloat16 [4, 4096, 2048], P(('section', 'dp'), 'ep'), may hold values from -1.5 to 1.5
- w_gate_up: bfloat16 [64, 2048, 1536], P(('section', 'ep')), may hold values from -0.125 to 0.125
- w_down: bfloat16 [64, 768, 2048], P(('section', 'ep')), may hold values from -0.21875 to 0.21875
Outputs:
- grad_x: bfloat16 [4, 4096, 2048], P(('section', 'dp'), 'ep')
- grad_w: bfloat16 [4, 4096, 8], P(('section', 'dp'), 'ep')
Inputs may be any that keep to these rules, and one draw needn't show every extreme that they name: `req_frames`: the 4 counts of each packed sequence sum to 128, and the largest of them is 64. `expert_ids`: the 8 experts of a token are distinct. Among the tokens of one packed sequence no expert is named more than 20 times, and in every draw some expert is named exactly 20 times there.
All inputs are finite; a program needn't handle non-finite values.
Results may differ from a plain program's by a relative error of at most 0.023.
Values may be sent and summed in bfloat16 or wider, within the bound.
A program may use at most 128 MiB of HBM per device.

v0:
```python
import math

import jax
import jax.numpy as jnp
import numpy as np
from jax import lax
from jax.experimental import pallas as pl
from jax.experimental.pallas import tpu as pltpu
from jax.sharding import PartitionSpec as P

NFFT = 400
HOP = 160
TIME = 64
MEL_FLOOR = 0.1
EPS_LAYER = 1e-05
EPS_ROOT = 1e-06
SAMPLE_RATE = 16000.0
CAP = 20
HEAD = 16
TAIL = CAP - HEAD
WIDTH = 2048
PART = WIDTH // 4
HIGHEST = lax.Precision.HIGHEST


def mel_scale(frequency):
    frequency = np.asarray(frequency) * 1.0
    log_part = 15.0 + np.log(np.maximum(frequency, 1000.0) / 1000.0) * 27.0 / math.log(6.4)
    return np.where(frequency < 1000.0, frequency * 3.0 / 200.0, log_part)


def mel_inverse(levels):
    levels = np.asarray(levels) * 1.0
    log_part = 1000.0 * np.exp((np.maximum(levels, 15.0) - 15.0) * math.log(6.4) / 27.0)
    return np.where(levels < 15.0, levels * 200.0 / 3.0, log_part)


def mel_table(bins_count, mel_count, frame_size):
    edges = mel_inverse(np.linspace(0.0, float(mel_scale(SAMPLE_RATE / 2.0)), mel_count + 2))
    centers = (np.arange(bins_count) * 1.0)[:, None] * SAMPLE_RATE / frame_size
    lower = edges[:-2][None, :]
    middle = edges[1:-1][None, :]
    upper = edges[2:][None, :]
    rising = (centers - lower) / (middle - lower)
    falling = (upper - centers) / (upper - middle)
    return np.maximum(0.0, np.minimum(rising, falling))


def dft_windowed(count, bins_count):
    sample = np.arange(count)[:, None]
    frequency = np.arange(bins_count)[None, :]
    angle = 2.0 * np.pi * ((sample * frequency) % count) / count
    window = (0.5 - 0.5 * np.cos(2.0 * np.pi * np.arange(count) / count))[:, None]
    table = np.zeros((count, 512))
    table[:, :bins_count] = window * np.cos(angle)
    table[:, 256 : 256 + bins_count] = -window * np.sin(angle)
    return table.astype(np.float32)


def sinusoid_table(count, width):
    half = width // 2
    rates = np.exp(-math.log(10000.0) * np.arange(half) / (half - 1))
    angles = np.arange(count)[:, None] * rates[None, :]
    return np.concatenate([np.sin(angles), np.cos(angles)], axis=1).astype(np.float32)


def layer_norm(values):
    centered = values - jnp.mean(values, axis=-1, keepdims=True)
    return centered * lax.rsqrt(jnp.mean(centered * centered, axis=-1, keepdims=True) + EPS_LAYER)


def normalize(values, gain):
    return values * lax.rsqrt(jnp.mean(values * values, axis=-1, keepdims=True) + EPS_ROOT) * gain


def dot(left, right):
    return jnp.dot(left, right, preferred_element_type=jnp.float32)


def swap(value):
    return lax.ppermute(value, "dp", [(0, 1), (1, 0)])


def exchange(rows):
    width = rows.shape[-1]
    out = lax.all_to_all(
        rows.reshape(-1, HEAD, width), ("section", "ep"), split_axis=0, concat_axis=0, tiled=True
    )
    return out.reshape(-1, width)


def quarter_of(shape, axis=0):
    return lax.rem(lax.broadcasted_iota(jnp.int32, shape, axis), HEAD) // TAIL


def pack_body(head_ref, tail_ref, values_ref, out_ref):
    out_ref[:, :WIDTH] = dot(head_ref[...], values_ref[...]).astype(jnp.bfloat16)
    quarter = quarter_of((head_ref.shape[0], PART))
    packed = jnp.zeros(quarter.shape, jnp.float32)
    for q in range(4):
        piece = dot(tail_ref[...], values_ref[:, q * PART : (q + 1) * PART])
        packed = jnp.where(quarter == q, piece, packed)
    out_ref[:, WIDTH:] = packed.astype(jnp.bfloat16)


def pack(head_picks, tail_picks, values):
    rows, tokens = head_picks.shape
    block = rows // 4
    return pl.pallas_call(
        pack_body,
        grid=(4,),
        in_specs=[
            pl.BlockSpec((block, tokens), lambda i: (i, 0)),
            pl.BlockSpec((block, tokens), lambda i: (i, 0)),
            pl.BlockSpec((tokens, WIDTH), lambda i: (0, 0)),
        ],
        out_specs=pl.BlockSpec((block, WIDTH + PART), lambda i: (i, 0)),
        out_shape=jax.ShapeDtypeStruct((rows, WIDTH + PART), jnp.bfloat16),
        cost_estimate=pl.CostEstimate(
            flops=4 * rows * tokens * WIDTH, bytes_accessed=6_500_000, transcendentals=0
        ),
        name="pack_slots",
    )(head_picks, tail_picks, values)


def contract_last(left, right):
    return lax.dot_general(
        left, right, (((1,), (1,)), ((), ())), preferred_element_type=jnp.float32
    )


def expert_body(rows_ref, grads_ref, gate_up_ref, down_ref, out_ref, full_ref):
    head = rows_ref.shape[0]
    tail = head // 4
    hidden_count = down_ref.shape[0]
    to = lax.broadcasted_iota(jnp.int32, (tail, head), 0)
    at = lax.broadcasted_iota(jnp.int32, (tail, head), 1)
    base = (to // TAIL) * HEAD + lax.rem(to, TAIL)

    def unpack(ref):
        full_ref[:head, :] = ref[:, :WIDTH]
        for q in range(4):
            gather = jnp.where(at == base + q * TAIL, 1.0, 0.0).astype(jnp.bfloat16)
            full_ref[head:, q * PART : (q + 1) * PART] = dot(gather, ref[:, WIDTH:]).astype(
                jnp.bfloat16
            )

    unpack(grads_ref)
    back = contract_last(full_ref[...], down_ref[...])
    unpack(rows_ref)
    both = dot(full_ref[...], gate_up_ref[...])
    gate = both[:, :hidden_count]
    upper = both[:, hidden_count:]
    sigma = jax.nn.sigmoid(gate)
    active = (gate * sigma * upper).astype(jnp.bfloat16).astype(jnp.float32)
    products = jnp.sum(active * back, axis=1, keepdims=True)
    d_gate = back * upper * sigma * (1.0 + gate * (1.0 - sigma))
    d_upper = back * gate * sigma
    d_both = jnp.concatenate([d_gate.astype(jnp.bfloat16), d_upper.astype(jnp.bfloat16)], axis=1)
    d_rows = contract_last(d_both, gate_up_ref[...]).astype(jnp.bfloat16)
    out_ref[:, :WIDTH] = d_rows[:head]
    row = lax.broadcasted_iota(jnp.int32, (head, tail), 0)
    column = lax.broadcasted_iota(jnp.int32, (head, tail), 1)
    source = (row // HEAD) * TAIL + lax.rem(row, TAIL)
    scatter = jnp.where(column == source, 1.0, 0.0).astype(jnp.bfloat16)
    quarter = quarter_of((head, PART))
    packed = jnp.zeros((head, PART), jnp.float32)
    for q in range(4):
        piece = dot(scatter, d_rows[head:, q * PART : (q + 1) * PART])
        packed = jnp.where(quarter == q, piece, packed)
    out_ref[:, WIDTH : WIDTH + PART] = packed.astype(jnp.bfloat16)
    wide = jnp.broadcast_to(products, (head + tail, 128))
    tail_wide = dot(scatter, wide[head:].astype(jnp.bfloat16))
    lane = lax.broadcasted_iota(jnp.int32, (head, 128), 1)
    out_ref[:, WIDTH + PART :] = jnp.where(lane < 64, wide[:head], tail_wide).astype(jnp.bfloat16)


def experts_run(rows, grads, gate_up, down):
    total = rows.shape[0]
    block = total // 4
    full = lambda i: (0, 0)
    return pl.pallas_call(
        expert_body,
        grid=(4,),
        in_specs=[
            pl.BlockSpec((block, WIDTH + PART), lambda i: (i, 0)),
            pl.BlockSpec((block, WIDTH + PART), lambda i: (i, 0)),
            pl.BlockSpec(gate_up.shape, full),
            pl.BlockSpec(down.shape, full),
        ],
        out_specs=pl.BlockSpec((block, WIDTH + PART + 128), lambda i: (i, 0)),
        out_shape=jax.ShapeDtypeStruct((total, WIDTH + PART + 128), jnp.bfloat16),
        scratch_shapes=[pltpu.VMEM((block + block // 4, WIDTH), jnp.bfloat16)],
        compiler_params=pltpu.CompilerParams(vmem_limit_bytes=62_000_000),
        cost_estimate=pl.CostEstimate(
            flops=20_000_000_000, bytes_accessed=25_000_000, transcendentals=1_000_000
        ),
        name="experts",
    )(rows, grads, gate_up, down)


def combine_body(head_ref, tail_ref, rows_ref, out_ref):
    tokens = out_ref.shape[0]

    def split(value):
        coarse = value.astype(jnp.bfloat16)
        fine = (value - coarse.astype(jnp.float32)).astype(jnp.bfloat16)
        return jnp.concatenate([coarse, fine], axis=0)

    head = split(head_ref[...])
    quarter = quarter_of(tail_ref.shape, 1)
    for q in range(4):
        columns = pl.ds(q * PART, PART)
        weights = split(jnp.where(quarter == q, tail_ref[...], 0.0))
        total = dot(head, rows_ref[:, columns]) + dot(weights, rows_ref[:, WIDTH : WIDTH + PART])
        out_ref[:, columns] = total[:tokens] + total[tokens:]


def combine(head_weights, tail_weights, rows):
    return pl.pallas_call(
        combine_body,
        out_shape=jax.ShapeDtypeStruct((head_weights.shape[0], WIDTH), jnp.float32),
        name="combine",
    )(head_weights, tail_weights, rows)


def shards(
    samples,
    req_frames,
    w_in,
    w_up_aud,
    w_down_aud,
    w_out,
    norm_gain,
    expert_ids,
    gate_weights,
    cotangent,
    w_gate_up,
    w_down,
):
    local_rows = samples[0]
    request_total, slab, hop = local_rows.shape
    grads = cotangent[0]
    tokens, width = grads.shape
    experts = lax.axis_size("section") * lax.axis_size("ep")
    senders = lax.axis_size("ep")
    requests = request_total // senders

    arrived = lax.all_to_all(
        local_rows.reshape(senders, requests * slab, hop),
        "ep",
        split_axis=0,
        concat_axis=0,
        tiled=True,
    ).reshape(-1, hop)

    ids = expert_ids[0].T
    names = ids[:, None, :] == jnp.arange(experts, dtype=jnp.int32)[None, :, None]
    member = jnp.any(names, axis=0)
    before = jnp.asarray(np.triu(np.ones((tokens, tokens)), 1), jnp.bfloat16)
    rank = dot(member.astype(jnp.bfloat16), before).astype(jnp.int32)
    rank = jnp.where(member, rank, -1)
    place = jnp.arange(HEAD, dtype=jnp.int32)[None, :, None]
    head_slots = (rank[:, None, :] == place).reshape(-1, tokens)
    tail_slots = (rank[:, None, :] == HEAD + place % TAIL).reshape(-1, tokens)
    head_picks = head_slots.astype(jnp.bfloat16)
    tail_picks = tail_slots.astype(jnp.bfloat16)
    arrived_grads = exchange(pack(head_picks, tail_picks, grads))

    lengths = req_frames[0, 0]
    ends = jnp.cumsum(lengths)
    places = jnp.arange(tokens, dtype=jnp.int32)
    later = places[:, None] >= ends[None, :-1]
    request = jnp.sum(later.astype(jnp.int32), axis=-1)
    times = places - jnp.sum(jnp.where(later, lengths[None, :-1], 0), axis=-1)
    parts = []
    for offset in range(3):
        at = times + offset
        row = jnp.where(at < TIME, (at // slab) * (requests * slab) + request * slab + at % slab, -1)
        pick = (row[:, None] == jnp.arange(arrived.shape[0], dtype=jnp.int32)).astype(jnp.float32)
        parts.append(jnp.dot(pick, arrived, precision=HIGHEST, preferred_element_type=jnp.float32))
    frames = jnp.concatenate(parts, axis=-1)[:, :NFFT]

    bins_count = NFFT // 2 + 1
    spectrum = jnp.dot(
        frames,
        jnp.asarray(dft_windowed(NFFT, bins_count)),
        precision=HIGHEST,
        preferred_element_type=jnp.float32,
    )
    power = spectrum[:, :256] ** 2 + spectrum[:, 256:] ** 2
    table = np.zeros((256, w_in.shape[0]), np.float32)
    table[:bins_count] = mel_table(bins_count, w_in.shape[0], NFFT)
    energy = jnp.dot(
        power, jnp.asarray(table), precision=HIGHEST, preferred_element_type=jnp.float32
    )
    log_mel = jnp.log(jnp.maximum(energy, MEL_FLOOR)).astype(jnp.bfloat16)
    time_pick = (times[:, None] == jnp.arange(TIME, dtype=jnp.int32)).astype(jnp.float32)
    position = jnp.dot(
        time_pick,
        jnp.asarray(sinusoid_table(TIME, w_in.shape[1])),
        precision=HIGHEST,
        preferred_element_type=jnp.float32,
    )
    state = dot(log_mel, w_in) + position
    normed_audio = layer_norm(state).astype(jnp.bfloat16)

    def half_product(values):
        hidden = jax.nn.gelu(dot(values, w_up_aud), approximate=False).astype(jnp.bfloat16)
        return dot(hidden, w_down_aud)

    other = swap(normed_audio)
    theirs = half_product(other).astype(jnp.bfloat16)
    ours = half_product(normed_audio)
    encoded = state + (ours + swap(theirs).astype(jnp.float32))
    final_audio = layer_norm(encoded).astype(jnp.bfloat16)
    values = dot(final_audio, w_out).astype(jnp.bfloat16).astype(jnp.float32)
    normed = normalize(values, norm_gain).astype(jnp.bfloat16)

    normed, arrived_grads = lax.optimization_barrier((normed, arrived_grads))
    arrived_rows = exchange(pack(head_picks, tail_picks, normed))
    returned = exchange(experts_run(arrived_rows, arrived_grads, w_gate_up[0], w_down[0]))

    weight = jnp.sum(jnp.where(names, gate_weights[0].T[:, None, :], 0.0), axis=0)
    weight = jnp.broadcast_to(weight[:, None, :], (experts, HEAD, tokens)).reshape(-1, tokens)
    d_normed = combine(
        jnp.where(head_slots, weight, 0.0).T, jnp.where(tail_slots, weight, 0.0).T, returned
    )
    d_values = jax.vjp(lambda inner: normalize(inner, norm_gain), values)[1](d_normed)[0]
    grad_x = (grads.astype(jnp.float32) + d_values).astype(jnp.bfloat16)

    scalars = returned[:, WIDTH + PART :].astype(jnp.float32)
    first = (jnp.arange(experts * HEAD) % HEAD < TAIL)[:, None]
    picked = jnp.where(head_slots, scalars[:, :1], 0.0)
    picked = picked + jnp.where(tail_slots & first, scalars[:, 64:65], 0.0)
    by_token = jnp.sum(picked.reshape(experts, HEAD, tokens), axis=1)
    grad_w = jnp.sum(jnp.where(names, by_token[None], 0.0), axis=1).T.astype(jnp.bfloat16)
    return (grad_x[None], grad_w[None])


def solution(mesh):
    in_specs = (
        P(("section", "dp"), None, "ep", None),
        P(("section", "dp"), "ep", None),
        P(),
        P(None, "dp"),
        P("dp", None),
        P(),
        P(),
        P(("section", "dp"), "ep", None),
        P(("section", "dp"), "ep", None),
        P(("section", "dp"), "ep", None),
        P(("section", "ep"), None, None),
        P(("section", "ep"), None, None),
    )
    out_specs = (P(("section", "dp"), "ep", None), P(("section", "dp"), "ep", None))
    return jax.shard_map(shards, mesh=mesh, in_specs=in_specs, out_specs=out_specs, check_vma=False)
```

profile of v0, /device:TPU:11, one launch (start us, length us, event | category | flops | bytes accessed | tf_op | source)
XLA Modules:
  0.0 346.8 jit_solution(214266605284459353)
XLA Ops:
  0.6 1.2 copy.36
  1.9 0.9 reshape_squeeze.3
  2.8 7.8 %all-to-all-start = ((f32[32,8,160]{2,1,0:T(8,128)}), f32[32,8,160]{2,1,0:T(8,128)S(1)}, u32[]{:S(2)}, u32[]{:S(2)}) async-start(f32[32,8,160]{2,1,0:T(8,128)} %reshape_squeeze.3), calls=%async_computation | async-start | bytes 524288 | tf_op jit(solution)/shard_map/all_to_all | solution.py:249
  13.3 0.9 fusion.3
  15.7 2.0 copy.32
  18.3 0.8 eq.129
  21.3 2.0 fusion.179
  23.9 1.8 copy.39.head_ref
  25.7 1.8 copy.40.tail_ref
  27.5 5.6 %pack_slots.2 = bf16[1024,2560]{1,0:T(8,128)(2,1)} custom-call(bf16[1024,128]{1,0:T(8,128)(2,1)} %copy.39.head_ref, bf16[1024,128]{1,0:T(8,128)(2,1)} %copy.40.tail_ref, bf16[128,2048]{1,0:T(8,128)(2,1)} %bitcast.59), custom_call_target="tpu_custom_call" | custom-call | flops 1073741824 | bytes 6500000 | tf_op jit(solution)/shard_map/pack_slots/pallas_call | solution.py:109
  33.1 11.3 %all-to-all-start.1 = ((bf16[64,16,2560]{2,1,0:T(8,128)(2,1)}), bf16[64,16,2560]{2,1,0:T(8,128)(2,1)}, u32[]{:S(2)}, u32[]{:S(2)}) async-start(bf16[64,16,2560]{2,1,0:T(8,128)(2,1)} %bitcast.55), calls=%async_computation.1 | async-start | bytes 10485760 | tf_op jit(solution)/shard_map/all_to_all | solution.py:86
  44.4 1.1 fusion.96
  46.3 1.9 fusion.101
  48.2 1.2 fusion.2
  49.4 1.2 fusion.187
  53.0 54.7 %collective-permute-done = bf16[128,1280]{1,0:T(8,128)(2,1)} collective-permute-done((bf16[128,1280]{1,0:T(8,128)(2,1)S(1)}, bf16[128,1280]{1,0:T(8,128)(2,1)}, u32[]{:S(2)}, u32[]{:S(2)}) %collective-permute-start) | collective-permute-done | bytes 327712 | tf_op jit(solution)/shard_map/ppermute | solution.py:81
  107.7 5.2 %convolution_convert_fusion.1 = bf16[128,1280]{1,0:T(8,128)(2,1)} fusion(bf16[1280,1280]{1,0:T(8,128)(2,1)S(1)} %copy-done, bf16[128,1280]{1,0:T(8,128)(2,1)} %collective-permute-done, bf16[1280,1280]{1,0:T(8,128)(2,1)} %param.19), kind=kOutput, calls=%fused_computation.3 | convolution fusion | flops 849674240 | bytes 7208960 | tf_op jit(solution)/shard_map/dot_general | solution.py:77
  113.6 9.3 %collective-permute-done.1 = bf16[128,1280]{1,0:T(8,128)(2,1)} collective-permute-done((bf16[128,1280]{1,0:T(8,128)(2,1)}, bf16[128,1280]{1,0:T(8,128)(2,1)}, u32[]{:S(2)}, u32[]{:S(2)}) %collective-permute-start.1) | collective-permute-done | bytes 327712 | tf_op jit(solution)/shard_map/ppermute | solution.py:81
  122.9 5.7 %fusion.182 = (f32[128]{0:T(128)S(1)}, f32[128,1280]{1,0:T(8,128)}) fusion(f32[128,1280]{1,0:T(8,128)} %copy-done.3, bf16[128,1280]{1,0:T(8,128)(2,1)} %collective-permute-done.1, bf16[1280,1280]{1,0:T(8,128)(2,1)S(1)} %copy-done, bf16[1280,1280]{1,0:T(8,128)(2,1)} %param.19, f32[128]{0:T(128)S(1)} %add_rsqrt_fusion.1, f32[128]{0:T(128)S(1)} %broadcast_multiply_fusion.1), kind=kOutput, calls=%fused_computation.264 | convolution fusion | flops 850657152 | bytes 8193536 | tf_op jit(solution)/shard_map/dot_general | solution.py:77
  128.6 1.3 multiply_reduce_fusion.2
  129.9 3.7 %multiply_reduce_fusion.1 = (f32[128]{0:T(128)S(1)}, f32[128,2048]{1,0:T(8,128)S(1)}) fusion(bf16[1280,2048]{1,0:T(8,128)(2,1)} %param.21, f32[128,1280]{1,0:T(8,128)} %get-tuple-element.27, f32[128]{0:T(128)S(1)} %add_rsqrt_fusion, f32[128]{0:T(128)S(1)} %broadcast_multiply_fusion), kind=kOutput, calls=%fused_computation.14 | convolution fusion | flops 672628608 | bytes 6948352 | tf_op jit(solution)/shard_map/dot_general | solution.py:77
  133.6 1.1 multiply_convert_fusion.values_ref
  134.8 5.6 %pack_slots.3 = bf16[1024,2560]{1,0:T(8,128)(2,1)} custom-call(bf16[1024,128]{1,0:T(8,128)(2,1)} %copy.39.head_ref, bf16[1024,128]{1,0:T(8,128)(2,1)} %copy.40.tail_ref, bf16[128,2048]{1,0:T(8,128)(2,1)} %multiply_convert_fusion.values_ref), custom_call_target="tpu_custom_call" | custom-call | flops 1073741824 | bytes 6500000 | tf_op jit(solution)/shard_map/pack_slots/pallas_call | solution.py:109
  140.4 76.1 %all_to_all.20 = bf16[64,16,2560]{2,1,0:T(8,128)(2,1)} all-to-all(bf16[64,16,2560]{2,1,0:T(8,128)(2,1)} %bitcast.56), channel_id=1, replica_groups=mesh['section'=2,'ep'=32,'dp'=2] {'section','ep'}, dimensions={0} | all-to-all | bytes 10485760 | tf_op jit(solution)/shard_map/all_to_all | solution.py:86
  216.5 31.1 %experts.1 = bf16[1024,2688]{1,0:T(8,128)(2,1)} custom-call(bf16[1024,2560]{1,0:T(8,128)(2,1)} %bitcast.58, bf16[1024,2560]{1,0:T(8,128)(2,1)} %bitcast.14.grads_ref, bf16[2048,1536]{1,0:T(8,128)(2,1)} %bitcast.66, bf16[768,2048]{1,0:T(8,128)(2,1)} %bitcast.67), custom_call_target="tpu_custom_call" | custom-call | flops 20000000000 | bytes 25000000 | tf_op jit(solution)/shard_map/experts/pallas_call | solution.py:182
  247.6 6.6 %all-to-all-start.3 = ((bf16[64,16,2688]{2,1,0:T(8,128)(2,1)}), bf16[64,16,2688]{2,1,0:T(8,128)(2,1)}, u32[]{:S(2)}, u32[]{:S(2)}) async-start(bf16[64,16,2688]{2,1,0:T(8,128)(2,1)} %bitcast.57), calls=%async_computation.3 | async-start | bytes 11010048 | tf_op jit(solution)/shard_map/all_to_all | solution.py:86
  254.2 77.4 %all-to-all-done.3 = bf16[64,16,2688]{2,1,0:T(8,128)(2,1)} async-done(((bf16[64,16,2688]{2,1,0:T(8,128)(2,1)}), bf16[64,16,2688]{2,1,0:T(8,128)(2,1)}, u32[]{:S(2)}, u32[]{:S(2)}) %all-to-all-start.3) | async-done | bytes 5505056 | tf_op jit(solution)/shard_map/all_to_all | solution.py:86
  331.7 1.0 slice_convert_fusion
  334.7 1.1 select_bitcast_fusion
  335.9 6.4 %combine.1 = f32[128,2048]{1,0:T(8,128)} custom-call(f32[128,1024]{1,0:T(8,128)} %get-tuple-element.17.head_ref, f32[128,1024]{1,0:T(8,128)} %get-tuple-element.16.tail_ref, bf16[1024,2688]{1,0:T(8,128)(2,1)} %bitcast.20.rows_ref), custom_call_target="tpu_custom_call" | custom-call | tf_op jit(solution)/shard_map/combine/pallas_call | solution.py:220
  342.2 1.7 multiply_reduce_fusion
  344.0 2.8 fusion.26
  (58 shorter events, 13.5 us)
Async XLA Ops:
  0.6 107.1 %copy-start = (bf16[1280,1280]{1,0:T(8,128)(2,1)S(1)}, bf16[1280,1280]{1,0:T(8,128)(2,1)}, u32[]{:S(2)}) copy-start(bf16[1280,1280]{1,0:T(8,128)(2,1)} %param.20) | copy-start | bytes 9830404
  2.8 30.3 %all-to-all-start = ((f32[32,8,160]{2,1,0:T(8,128)}), f32[32,8,160]{2,1,0:T(8,128)S(1)}, u32[]{:S(2)}, u32[]{:S(2)}) async-start(f32[32,8,160]{2,1,0:T(8,128)} %reshape_squeeze.3), calls=%async_computation | async-start | bytes 524288 | tf_op jit(solution)/shard_map/all_to_all | solution.py:249
  14.2 0.6 copy-start.7
  33.1 101.7 %all-to-all-start.1 = ((bf16[64,16,2560]{2,1,0:T(8,128)(2,1)}), bf16[64,16,2560]{2,1,0:T(8,128)(2,1)}, u32[]{:S(2)}, u32[]{:S(2)}) async-start(bf16[64,16,2560]{2,1,0:T(8,128)(2,1)} %bitcast.55), calls=%async_computation.1 | async-start | bytes 10485760 | tf_op jit(solution)/shard_map/all_to_all | solution.py:86
  44.4 6.2 %copy-start.6 = (f32[64,1280]{1,0:T(8,128)S(1)}, f32[64,1280]{1,0:T(8,128)}, u32[]{:S(2)}) copy-start(f32[64,1280]{1,0:T(8,128)} %constant.186.clone) | copy-start | bytes 983044
  51.1 0.9 copy-start.3
  52.2 55.5 %collective-permute-start = (bf16[128,1280]{1,0:T(8,128)(2,1)S(1)}, bf16[128,1280]{1,0:T(8,128)(2,1)}, u32[]{:S(2)}, u32[]{:S(2)}) collective-permute-start(bf16[128,1280]{1,0:T(8,128)(2,1)S(1)} %multiply_convert_fusion.2), channel_id=1, source_target_pairs={{0,1},{1,0},{2,3},{3,2},{4,5},{5,4},{6,7},{7,6},{8,9},{9,8},{10,11... | collective-permute-start | bytes 983048 | tf_op jit(solution)/shard_map/ppermute | solution.py:81
  112.9 10.0 %collective-permute-start.1 = (bf16[128,1280]{1,0:T(8,128)(2,1)}, bf16[128,1280]{1,0:T(8,128)(2,1)}, u32[]{:S(2)}, u32[]{:S(2)}) collective-permute-start(bf16[128,1280]{1,0:T(8,128)(2,1)} %convolution_convert_fusion.1), channel_id=1, source_target_pairs={{0,1},{1,0},{2,3},{3,2},{4,5},{5,4},{6,7},{7,6},{8,9},{9,8},{10,11... | collective-permute-start | bytes 983048 | tf_op jit(solution)/shard_map/ppermute | solution.py:81
  129.9 3.7 %copy-start.9 = (f32[2048]{0:T(1024)S(1)}, f32[2048]{0:T(1024)}, u32[]{:S(2)}) copy-start(f32[2048]{0:T(1024)} %param.22) | copy-start | bytes 24580
  133.6 6.8 %copy-start.2 = (f32[128,2048]{1,0:T(8,128)}, f32[128,2048]{1,0:T(8,128)S(1)}, u32[]{:S(2)}) copy-start(f32[128,2048]{1,0:T(8,128)S(1)} %get-tuple-element.29) | copy-start | bytes 3145732
  247.6 85.7 %copy-start.8 = (s32[64,128]{1,0:T(8,128)S(1)}, s32[64,128]{1,0:T(8,128)}, u32[]{:S(2)}) copy-start(s32[64,128]{1,0:T(8,128)} %copy-done.7) | copy-start | bytes 98308
  247.6 86.2 %copy-start.10 = (s32[1,128,8]{1,2,0:T(8,128)S(1)}, s32[1,128,8]{1,2,0:T(8,128)}, u32[]{:S(2)}) copy-start(s32[1,128,8]{1,2,0:T(8,128)} %param.23) | copy-start | bytes 12292
  247.6 86.2 %copy-start.11 = (f32[1,128,8]{1,2,0:T(8,128)S(1)}, f32[1,128,8]{1,2,0:T(8,128)}, u32[]{:S(2)}) copy-start(f32[1,128,8]{1,2,0:T(8,128)} %param.24) | copy-start | bytes 12292
  247.6 84.1 %all-to-all-start.3 = ((bf16[64,16,2688]{2,1,0:T(8,128)(2,1)}), bf16[64,16,2688]{2,1,0:T(8,128)(2,1)}, u32[]{:S(2)}, u32[]{:S(2)}) async-start(bf16[64,16,2688]{2,1,0:T(8,128)(2,1)} %bitcast.57), calls=%async_computation.3 | async-start | bytes 11010048 | tf_op jit(solution)/shard_map/all_to_all | solution.py:86
  254.2 80.5 %copy-start.4 = (pred[1024,128]{0,1:T(8,128)(4,1)S(1)}, pred[1024,128]{0,1:T(8,128)(4,1)}, u32[]{:S(2)}) copy-start(pred[1024,128]{0,1:T(8,128)(4,1)} %get-tuple-element.13) | copy-start | bytes 393220
  254.2 80.5 %copy-start.5 = (pred[1024,128]{0,1:T(8,128)(4,1)S(1)}, pred[1024,128]{0,1:T(8,128)(4,1)}, u32[]{:S(2)}) copy-start(pred[1024,128]{0,1:T(8,128)(4,1)} %get-tuple-element.19) | copy-start | bytes 393220
  335.9 10.9 %copy-start.1 = (bf16[1280,1280]{1,0:T(8,128)(2,1)S(1)}, bf16[1280,1280]{1,0:T(8,128)(2,1)}, u32[]{:S(2)}) copy-start(bf16[1280,1280]{1,0:T(8,128)(2,1)} %param.20) | copy-start | bytes 9830404
where the time goes:
time: 348 us; the launch traced here: 347 us
  waiting for transfers between devices  141 us (41%)
  blocking collectives  76.1 us (22%)
  Pallas kernels  48.7 us (14%)
  starting transfers between devices  27.2 us (8%)
  matrix products  22.2 us (6%)
  other arithmetic  15.5 us (4%)
  local copies, waits for them, and re-layouts  14.8 us (4%)
    all_to_all x2, waiting for transfers between devices, exchange(): lax.all_to_all(rows.reshape(-1, HEAD, width), ('section', 'ep'), split_ax...  77.4 us
    all_to_all x1, blocking collectives, exchange(): lax.all_to_all(rows.reshape(-1, HEAD, width), ('section', 'ep'), split_ax...  76.1 us
    ppermute x2, waiting for transfers between devices, swap(): return lax.ppermute(value, 'dp', [(0, 1), (1, 0)])  64 us
    pallas_call x1, Pallas kernels, experts_run(): pl.pallas_call(expert_body, grid=(4,), in_specs=[pl.BlockSpec((block, WID...  31.1 us
    all_to_all x2, starting transfers between devices, exchange(): lax.all_to_all(rows.reshape(-1, HEAD, width), ('section', 'ep'), split_ax...  17.8 us
    dot_general x5, matrix products, dot(): return jnp.dot(left, right, preferred_element_type=jnp.float32)  16.6 us
    pallas_call x2, Pallas kernels, pack(): pl.pallas_call(pack_body, grid=(4,), in_specs=[pl.BlockSpec((block, token...  11.2 us
    all_to_all x1, starting transfers between devices, shards(): lax.all_to_all(local_rows.reshape(senders, requests * slab, hop), 'ep', s...  7.83 us
  transfers between devices with their start and end apart: 5, of which 3 were waited for; matrix products, arithmetic and copies ran while one was open for 12% of the time, Pallas kernels for 2%

commit v1 on v0

--- a/solution.py
+++ b/solution.py
@@ -1,3 +1,4 @@
+import functools
 import math
 
 import jax
@@ -20,6 +21,7 @@
 TAIL = CAP - HEAD
 WIDTH = 2048
 PART = WIDTH // 4
+SPLIT = 1024
 HIGHEST = lax.Precision.HIGHEST
 
 
@@ -93,29 +95,33 @@
     return lax.rem(lax.broadcasted_iota(jnp.int32, shape, axis), HEAD) // TAIL
 
 
-def pack_body(head_ref, tail_ref, values_ref, out_ref):
-    out_ref[:, :WIDTH] = dot(head_ref[...], values_ref[...]).astype(jnp.bfloat16)
+def pack_body(split, head_ref, tail_ref, values_ref, *out_refs):
+    head = dot(head_ref[...], values_ref[...]).astype(jnp.bfloat16)
     quarter = quarter_of((head_ref.shape[0], PART))
     packed = jnp.zeros(quarter.shape, jnp.float32)
     for q in range(4):
         piece = dot(tail_ref[...], values_ref[:, q * PART : (q + 1) * PART])
         packed = jnp.where(quarter == q, piece, packed)
-    out_ref[:, WIDTH:] = packed.astype(jnp.bfloat16)
-
-
-def pack(head_picks, tail_picks, values):
+    if split:
+        out_refs[0][...] = head[:, :split]
+    out_refs[-1][:, : WIDTH - split] = head[:, split:]
+    out_refs[-1][:, WIDTH - split :] = packed.astype(jnp.bfloat16)
+
+
+def pack(head_picks, tail_picks, values, split=0):
     rows, tokens = head_picks.shape
     block = rows // 4
+    widths = ([split] if split else []) + [WIDTH + PART - split]
     return pl.pallas_call(
-        pack_body,
+        functools.partial(pack_body, split),
         grid=(4,),
         in_specs=[
             pl.BlockSpec((block, tokens), lambda i: (i, 0)),
             pl.BlockSpec((block, tokens), lambda i: (i, 0)),
             pl.BlockSpec((tokens, WIDTH), lambda i: (0, 0)),
         ],
-        out_specs=pl.BlockSpec((block, WIDTH + PART), lambda i: (i, 0)),
-        out_shape=jax.ShapeDtypeStruct((rows, WIDTH + PART), jnp.bfloat16),
+        out_specs=[pl.BlockSpec((block, width), lambda i: (i, 0)) for width in widths],
+        out_shape=[jax.ShapeDtypeStruct((rows, width), jnp.bfloat16) for width in widths],
         cost_estimate=pl.CostEstimate(
             flops=4 * rows * tokens * WIDTH, bytes_accessed=6_500_000, transcendentals=0
         ),
@@ -129,25 +135,54 @@
     )
 
 
-def expert_body(rows_ref, grads_ref, gate_up_ref, down_ref, out_ref, full_ref):
-    head = rows_ref.shape[0]
+def unpack_tail(packed, full_ref):
+    head = packed.shape[0]
     tail = head // 4
-    hidden_count = down_ref.shape[0]
     to = lax.broadcasted_iota(jnp.int32, (tail, head), 0)
     at = lax.broadcasted_iota(jnp.int32, (tail, head), 1)
     base = (to // TAIL) * HEAD + lax.rem(to, TAIL)
-
-    def unpack(ref):
-        full_ref[:head, :] = ref[:, :WIDTH]
-        for q in range(4):
-            gather = jnp.where(at == base + q * TAIL, 1.0, 0.0).astype(jnp.bfloat16)
-            full_ref[head:, q * PART : (q + 1) * PART] = dot(gather, ref[:, WIDTH:]).astype(
-                jnp.bfloat16
-            )
-
-    unpack(grads_ref)
-    back = contract_last(full_ref[...], down_ref[...])
-    unpack(rows_ref)
+    for q in range(4):
+        gather = jnp.where(at == base + q * TAIL, 1.0, 0.0).astype(jnp.bfloat16)
+        full_ref[head:, q * PART : (q + 1) * PART] = dot(gather, packed).astype(jnp.bfloat16)
+
+
+def back_body(first_ref, second_ref, down_ref, out_ref, full_ref):
+    head = first_ref.shape[0]
+    full_ref[:head, :SPLIT] = first_ref[...]
+    full_ref[:head, SPLIT:] = second_ref[:, : WIDTH - SPLIT]
+    unpack_tail(second_ref[:, WIDTH - SPLIT :], full_ref)
+    out_ref[...] = contract_last(full_ref[...], down_ref[...])
+
+
+def back_run(first, second, down):
+    total = first.shape[0]
+    block = total // 4
+    rows = block + block // 4
+    return pl.pallas_call(
+        back_body,
+        grid=(4,),
+        in_specs=[
+            pl.BlockSpec((block, first.shape[1]), lambda i: (i, 0)),
+            pl.BlockSpec((block, second.shape[1]), lambda i: (i, 0)),
+            pl.BlockSpec(down.shape, lambda i: (0, 0)),
+        ],
+        out_specs=pl.BlockSpec((rows, down.shape[0]), lambda i: (i, 0)),
+        out_shape=jax.ShapeDtypeStruct((4 * rows, down.shape[0]), jnp.float32),
+        scratch_shapes=[pltpu.VMEM((rows, WIDTH), jnp.bfloat16)],
+        cost_estimate=pl.CostEstimate(
+            flops=4_500_000_000, bytes_accessed=13_000_000, transcendentals=0
+        ),
+        name="back",
+    )(first, second, down)
+
+
+def expert_body(rows_ref, back_ref, gate_up_ref, out_ref, full_ref):
+    head = rows_ref.shape[0]
+    tail = head // 4
+    hidden_count = back_ref.shape[1]
+    back = back_ref[...]
+    full_ref[:head, :] = rows_ref[:, :WIDTH]
+    unpack_tail(rows_ref[:, WIDTH:], full_ref)
     both = dot(full_ref[...], gate_up_ref[...])
     gate = both[:, :hidden_count]
     upper = both[:, hidden_count:]
@@ -175,7 +210,7 @@
     out_ref[:, WIDTH + PART :] = jnp.where(lane < 64, wide[:head], tail_wide).astype(jnp.bfloat16)
 
 
-def experts_run(rows, grads, gate_up, down):
+def experts_run(rows, back, gate_up):
     total = rows.shape[0]
     block = total // 4
     full = lambda i: (0, 0)
@@ -184,19 +219,18 @@
         grid=(4,),
         in_specs=[
             pl.BlockSpec((block, WIDTH + PART), lambda i: (i, 0)),
-            pl.BlockSpec((block, WIDTH + PART), lambda i: (i, 0)),
+            pl.BlockSpec((block + block // 4, back.shape[1]), lambda i: (i, 0)),
             pl.BlockSpec(gate_up.shape, full),
-            pl.BlockSpec(down.shape, full),
         ],
         out_specs=pl.BlockSpec((block, WIDTH + PART + 128), lambda i: (i, 0)),
         out_shape=jax.ShapeDtypeStruct((total, WIDTH + PART + 128), jnp.bfloat16),
         scratch_shapes=[pltpu.VMEM((block + block // 4, WIDTH), jnp.bfloat16)],
         compiler_params=pltpu.CompilerParams(vmem_limit_bytes=62_000_000),
         cost_estimate=pl.CostEstimate(
-            flops=20_000_000_000, bytes_accessed=25_000_000, transcendentals=1_000_000
+            flops=16_000_000_000, bytes_accessed=25_000_000, transcendentals=1_000_000
         ),
         name="experts",
-    )(rows, grads, gate_up, down)
+    )(rows, back, gate_up)
 
 
 def combine_body(head_ref, tail_ref, rows_ref, out_ref):
@@ -209,8 +243,10 @@
 
     head = split(head_ref[...])
     quarter = quarter_of(tail_ref.shape, 1)
-    for q in range(4):
-        columns = pl.ds(q * PART, PART)
+
+    @pl.loop(0, 4)
+    def _(q):
+        columns = pl.ds(pl.multiple_of(q * PART, PART), PART)
         weights = split(jnp.where(quarter == q, tail_ref[...], 0.0))
         total = dot(head, rows_ref[:, columns]) + dot(weights, rows_ref[:, WIDTH : WIDTH + PART])
         out_ref[:, columns] = total[:tokens] + total[tokens:]
@@ -265,7 +301,8 @@
     tail_slots = (rank[:, None, :] == HEAD + place % TAIL).reshape(-1, tokens)
     head_picks = head_slots.astype(jnp.bfloat16)
     tail_picks = tail_slots.astype(jnp.bfloat16)
-    arrived_grads = exchange(pack(head_picks, tail_picks, grads))
+    grads_first, grads_second = pack(head_picks, tail_picks, grads, SPLIT)
+    arrived_first = exchange(grads_first)
 
     lengths = req_frames[0, 0]
     ends = jnp.cumsum(lengths)
@@ -309,17 +346,23 @@
         hidden = jax.nn.gelu(dot(values, w_up_aud), approximate=False).astype(jnp.bfloat16)
         return dot(hidden, w_down_aud)
 
+    normed_audio, arrived_first = lax.optimization_barrier((normed_audio, arrived_first))
     other = swap(normed_audio)
     theirs = half_product(other).astype(jnp.bfloat16)
     ours = half_product(normed_audio)
-    encoded = state + (ours + swap(theirs).astype(jnp.float32))
+    added = swap(theirs)
+    grads_second, added = lax.optimization_barrier((grads_second, added))
+    arrived_second = exchange(grads_second)
+    encoded = state + (ours + added.astype(jnp.float32))
     final_audio = layer_norm(encoded).astype(jnp.bfloat16)
     values = dot(final_audio, w_out).astype(jnp.bfloat16).astype(jnp.float32)
     normed = normalize(values, norm_gain).astype(jnp.bfloat16)
 
-    normed, arrived_grads = lax.optimization_barrier((normed, arrived_grads))
-    arrived_rows = exchange(pack(head_picks, tail_picks, normed))
-    returned = exchange(experts_run(arrived_rows, arrived_grads, w_gate_up[0], w_down[0]))
+    (packed,) = pack(head_picks, tail_picks, normed)
+    packed, arrived_second = lax.optimization_barrier((packed, arrived_second))
+    arrived_rows = exchange(packed)
+    back = back_run(arrived_first, arrived_second, w_down[0])
+    returned = exchange(experts_run(arrived_rows, back, w_gate_up[0]))
 
     weight = jnp.sum(jnp.where(names, gate_weights[0].T[:, None, :], 0.0), axis=0)
     weight = jnp.broadcast_to(weight[:, None, :], (experts, HEAD, tokens)).reshape(-1, tokens)

time: 348 us -> 355 us (1.020)
  blocking collectives: 76.1 us -> 0 us
  waiting for transfers between devices: 141 us -> 207 us
  starting transfers between devices: 27.2 us -> 40.7 us
    all_to_all x2 -> x4, waiting for transfers between devices: 77.4 us -> 190 us  [exchange(): lax.all_to_all(rows.reshape(-1, HEAD, width), ('section', 'ep'), split_ax...]
    all_to_all x1 -> x0, blocking collectives: 76.1 us -> none  [exchange(): lax.all_to_all(rows.reshape(-1, HEAD, width), ('section', 'ep'), split_ax...]
    ppermute x2, waiting for transfers between devices: 64 us -> 16.8 us  [swap(): return lax.ppermute(value, 'dp', [(0, 1), (1, 0)])]
    all_to_all x2 -> x4, starting transfers between devices: 17.8 us -> 31.4 us  [exchange(): lax.all_to_all(rows.reshape(-1, HEAD, width), ('section', 'ep'), split_ax...]
    pallas_call x2 -> x3, Pallas kernels: 11.2 us -> 20.2 us  [the longest x2 11 us: pack(): pl.pallas_call(functools.partial(pack_body, split), grid=(4,), in_specs=[...]
    pallas_call x1, Pallas kernels: 31.1 us -> 24.7 us  [experts_run(): pl.pallas_call(expert_body, grid=(4,), in_specs=[pl.BlockSpec((block, WID...]
  transfers between devices with their start and end apart: 5 -> 7, of which waited for: 3 -> 6; matrix products, arithmetic and copies ran while one was open for 12% -> 10% of each run, Pallas kernels for 2% -> 6%
where the time goes in v1:
time: 355 us; the launch traced here: 353 us
  waiting for transfers between devices  207 us (58%)
  Pallas kernels  51.8 us (15%)
  starting transfers between devices  40.7 us (11%)
  matrix products  21.6 us (6%)
  other arithmetic  16.7 us (5%)
  local copies, waits for them, and re-layouts  14.8 us (4%)
    all_to_all x4, waiting for transfers between devices, exchange(): lax.all_to_all(rows.reshape(-1, HEAD, width), ('section', 'ep'), split_ax...  190 us
    all_to_all x4, starting transfers between devices, exchange(): lax.all_to_all(rows.reshape(-1, HEAD, width), ('section', 'ep'), split_ax...  31.4 us
    pallas_call x1, Pallas kernels, experts_run(): pl.pallas_call(expert_body, grid=(4,), in_specs=[pl.BlockSpec((block, WID...  24.7 us
    ppermute x2, waiting for transfers between devices, swap(): return lax.ppermute(value, 'dp', [(0, 1), (1, 0)])  16.8 us
    dot_general x5, matrix products, dot(): return jnp.dot(left, right, preferred_element_type=jnp.float32)  16 us
    pallas_call x2, Pallas kernels, pack(): pl.pallas_call(functools.partial(pack_body, split), grid=(4,), in_specs=[...  11 us
    pallas_call x1, Pallas kernels, back_run(): pl.pallas_call(back_body, grid=(4,), in_specs=[pl.BlockSpec((block, first...  9.21 us
    all_to_all x1, starting transfers between devices, shards(): lax.all_to_all(local_rows.reshape(senders, requests * slab, hop), 'ep', s...  7.83 us
  transfers between devices with their start and end apart: 7, of which 6 were waited for; matrix products, arithmetic and copies ran while one was open for 10% of the time, Pallas kernels for 6%

profile of v1, /device:TPU:11, one launch (start us, length us, event | category | flops | bytes accessed | tf_op | source)
XLA Modules:
  0.0 353.2 jit_solution(17689632965117673432)
XLA Ops:
  0.6 1.2 copy.36
  2.8 7.8 %all-to-all-start = ((f32[32,8,160]{2,1,0:T(8,128)}), f32[32,8,160]{2,1,0:T(8,128)S(1)}, u32[]{:S(2)}, u32[]{:S(2)}) async-start(f32[32,8,160]{2,1,0:T(8,128)} %reshape_squeeze.3), calls=%async_computation | async-start | bytes 524288 | tf_op jit(solution)/shard_map/all_to_all | solution.py:285
  15.7 2.0 copy.32
  21.3 2.0 fusion.178
  23.9 1.8 copy.39.head_ref
  25.7 1.8 copy.40.tail_ref
  27.5 5.3 %pack_slots.2 = (bf16[1024,1024]{1,0:T(8,128)(2,1)}, bf16[1024,1536]{1,0:T(8,128)(2,1)}) custom-call(bf16[1024,128]{1,0:T(8,128)(2,1)} %copy.39.head_ref, bf16[1024,128]{1,0:T(8,128)(2,1)} %copy.40.tail_ref, bf16[128,2048]{1,0:T(8,128)(2,1)} %bitcast.63), custom_call_target="tpu_custom_call" | custom-call | flops 1073741824 | bytes 6500000 | tf_op jit(solution)/shard_map/pack_slots/pallas_call | solution.py:115
  32.8 11.3 %all-to-all-start.1 = ((bf16[64,16,1024]{2,1,0:T(8,128)(2,1)}), bf16[64,16,1024]{2,1,0:T(8,128)(2,1)}, u32[]{:S(2)}, u32[]{:S(2)}) async-start(bf16[64,16,1024]{2,1,0:T(8,128)(2,1)} %bitcast.60), calls=%async_computation.1 | async-start | bytes 4194304 | tf_op jit(solution)/shard_map/all_to_all | solution.py:88
  46.0 1.9 fusion.99
  47.9 1.2 fusion.2
  49.1 1.2 fusion.185
  52.6 20.2 %all-to-all-done.1 = bf16[64,16,1024]{2,1,0:T(8,128)(2,1)} async-done(((bf16[64,16,1024]{2,1,0:T(8,128)(2,1)}), bf16[64,16,1024]{2,1,0:T(8,128)(2,1)}, u32[]{:S(2)}, u32[]{:S(2)}) %all-to-all-start.1) | async-done | bytes 2097184 | tf_op jit(solution)/shard_map/all_to_all | solution.py:88
  73.5 8.8 %collective-permute-done = bf16[128,1280]{1,0:T(8,128)(2,1)} collective-permute-done((bf16[128,1280]{1,0:T(8,128)(2,1)}, bf16[128,1280]{1,0:T(8,128)(2,1)}, u32[]{:S(2)}, u32[]{:S(2)}) %collective-permute-start) | collective-permute-done | bytes 327712 | tf_op jit(solution)/shard_map/ppermute | solution.py:83
  82.3 5.2 %convolution_convert_fusion.1 = bf16[128,1280]{1,0:T(8,128)(2,1)} fusion(bf16[1280,1280]{1,0:T(8,128)(2,1)S(1)} %copy-done, bf16[128,1280]{1,0:T(8,128)(2,1)} %collective-permute-done, bf16[1280,1280]{1,0:T(8,128)(2,1)} %param.19), kind=kOutput, calls=%fused_computation.3 | convolution fusion | flops 849674240 | bytes 7208960 | tf_op jit(solution)/shard_map/dot_general | solution.py:79
  88.2 7.9 %collective-permute-done.1 = bf16[128,1280]{1,0:T(8,128)(2,1)} collective-permute-done((bf16[128,1280]{1,0:T(8,128)(2,1)}, bf16[128,1280]{1,0:T(8,128)(2,1)}, u32[]{:S(2)}, u32[]{:S(2)}) %collective-permute-start.1) | collective-permute-done | bytes 327712 | tf_op jit(solution)/shard_map/ppermute | solution.py:83
  96.2 7.3 %all-to-all-start.2 = ((bf16[64,16,1536]{2,1,0:T(8,128)(2,1)}), bf16[64,16,1536]{2,1,0:T(8,128)(2,1)}, u32[]{:S(2)}, u32[]{:S(2)}) async-start(bf16[64,16,1536]{2,1,0:T(8,128)(2,1)} %bitcast.59), calls=%async_computation.2 | async-start | bytes 6291456 | tf_op jit(solution)/shard_map/all_to_all | solution.py:88
  103.5 5.3 %fusion.28 = f32[128,1280]{1,0:T(8,128)} fusion(bf16[1280,1280]{1,0:T(8,128)(2,1)S(1)} %copy-done, bf16[128,1280]{1,0:T(8,128)(2,1)} %multiply_convert_fusion.2, bf16[1280,1280]{1,0:T(8,128)(2,1)} %param.19), kind=kOutput, calls=%fused_computation.65 | convolution fusion | flops 849510400 | bytes 7536640 | tf_op jit(solution)/shard_map/dot_general | solution.py:79
  108.8 1.5 fusion.177
  110.6 3.5 multiply_reduce_fusion.1
  114.1 1.1 multiply_convert_fusion.values_ref
  115.2 5.7 %pack_slots.3 = bf16[1024,2560]{1,0:T(8,128)(2,1)} custom-call(bf16[1024,128]{1,0:T(8,128)(2,1)} %copy.39.head_ref, bf16[1024,128]{1,0:T(8,128)(2,1)} %copy.40.tail_ref, bf16[128,2048]{1,0:T(8,128)(2,1)} %multiply_convert_fusion.values_ref), custom_call_target="tpu_custom_call" | custom-call | flops 1073741824 | bytes 6500000 | tf_op jit(solution)/shard_map/pack_slots/pallas_call | solution.py:115
  120.9 27.6 %all-to-all-done.2 = bf16[64,16,1536]{2,1,0:T(8,128)(2,1)} async-done(((bf16[64,16,1536]{2,1,0:T(8,128)(2,1)}), bf16[64,16,1536]{2,1,0:T(8,128)(2,1)}, u32[]{:S(2)}, u32[]{:S(2)}) %all-to-all-start.2) | async-done | bytes 3145760 | tf_op jit(solution)/shard_map/all_to_all | solution.py:88
  148.5 6.0 %all-to-all-start.3 = ((bf16[64,16,2560]{2,1,0:T(8,128)(2,1)}), bf16[64,16,2560]{2,1,0:T(8,128)(2,1)}, u32[]{:S(2)}, u32[]{:S(2)}) async-start(bf16[64,16,2560]{2,1,0:T(8,128)(2,1)} %bitcast.57), calls=%async_computation.3 | async-start | bytes 10485760 | tf_op jit(solution)/shard_map/all_to_all | solution.py:88
  154.4 9.2 %back.1.back_ref = f32[1280,768]{1,0:T(8,128)} custom-call(bf16[1024,1024]{1,0:T(8,128)(2,1)} %bitcast.14.first_ref, bf16[1024,1536]{1,0:T(8,128)(2,1)} %bitcast.16.second_ref, bf16[768,2048]{1,0:T(8,128)(2,1)} %bitcast.69), custom_call_target="tpu_custom_call" | custom-call | flops 4499999744 | bytes 13000000 | tf_op jit(solution)/shard_map/back/pallas_call | solution.py:161
  163.6 64.7 %all-to-all-done.3 = bf16[64,16,2560]{2,1,0:T(8,128)(2,1)} async-done(((bf16[64,16,2560]{2,1,0:T(8,128)(2,1)}), bf16[64,16,2560]{2,1,0:T(8,128)(2,1)}, u32[]{:S(2)}, u32[]{:S(2)}) %all-to-all-start.3) | async-done | bytes 5242912 | tf_op jit(solution)/shard_map/all_to_all | solution.py:88
  228.4 24.7 %experts.1 = bf16[1024,2688]{1,0:T(8,128)(2,1)} custom-call(bf16[1024,2560]{1,0:T(8,128)(2,1)} %bitcast.18.rows_ref, f32[1280,768]{1,0:T(8,128)} %back.1.back_ref, bf16[2048,1536]{1,0:T(8,128)(2,1)} %bitcast.68), custom_call_target="tpu_custom_call" | custom-call | flops 16000000000 | bytes 25000000 | tf_op jit(solution)/shard_map/experts/pallas_call | solution.py:217
  253.1 6.8 %all-to-all-start.4 = ((bf16[64,16,2688]{2,1,0:T(8,128)(2,1)}), bf16[64,16,2688]{2,1,0:T(8,128)(2,1)}, u32[]{:S(2)}, u32[]{:S(2)}) async-start(bf16[64,16,2688]{2,1,0:T(8,128)(2,1)} %bitcast.58), calls=%async_computation.4 | async-start | bytes 11010048 | tf_op jit(solution)/shard_map/all_to_all | solution.py:88
  259.9 77.4 %all-to-all-done.4 = bf16[64,16,2688]{2,1,0:T(8,128)(2,1)} async-done(((bf16[64,16,2688]{2,1,0:T(8,128)(2,1)}), bf16[64,16,2688]{2,1,0:T(8,128)(2,1)}, u32[]{:S(2)}, u32[]{:S(2)}) %all-to-all-start.4) | async-done | bytes 5505056 | tf_op jit(solution)/shard_map/all_to_all | solution.py:88
  340.4 1.1 select_bitcast_fusion
  341.6 7.0 %combine.1 = f32[128,2048]{1,0:T(8,128)} custom-call(f32[128,1024]{1,0:T(8,128)} %get-tuple-element.31.head_ref, f32[128,1024]{1,0:T(8,128)} %get-tuple-element.30.tail_ref, bf16[1024,2688]{1,0:T(8,128)(2,1)} %bitcast.22.rows_ref), custom_call_target="tpu_custom_call" | custom-call | tf_op jit(solution)/shard_map/combine/pallas_call | solution.py:256
  348.6 1.7 multiply_reduce_fusion
  350.3 2.8 fusion.26
  (63 shorter events, 19.1 us)
Async XLA Ops:
  0.6 81.7 %copy-start = (bf16[1280,1280]{1,0:T(8,128)(2,1)S(1)}, bf16[1280,1280]{1,0:T(8,128)(2,1)}, u32[]{:S(2)}) copy-start(bf16[1280,1280]{1,0:T(8,128)(2,1)} %param.20) | copy-start | bytes 9830404
  2.8 30.1 %all-to-all-start = ((f32[32,8,160]{2,1,0:T(8,128)}), f32[32,8,160]{2,1,0:T(8,128)S(1)}, u32[]{:S(2)}, u32[]{:S(2)}) async-start(f32[32,8,160]{2,1,0:T(8,128)} %reshape_squeeze.3), calls=%async_computation | async-start | bytes 524288 | tf_op jit(solution)/shard_map/all_to_all | solution.py:285
  14.2 0.6 copy-start.7
  32.8 39.9 %all-to-all-start.1 = ((bf16[64,16,1024]{2,1,0:T(8,128)(2,1)}), bf16[64,16,1024]{2,1,0:T(8,128)(2,1)}, u32[]{:S(2)}, u32[]{:S(2)}) async-start(bf16[64,16,1024]{2,1,0:T(8,128)(2,1)} %bitcast.60), calls=%async_computation.1 | async-start | bytes 4194304 | tf_op jit(solution)/shard_map/all_to_all | solution.py:88
  44.1 6.2 %copy-start.6 = (f32[64,1280]{1,0:T(8,128)S(1)}, f32[64,1280]{1,0:T(8,128)}, u32[]{:S(2)}) copy-start(f32[64,1280]{1,0:T(8,128)} %constant.186.clone) | copy-start | bytes 983044
  50.9 0.8 copy-start.3
  72.7 9.6 %collective-permute-start = (bf16[128,1280]{1,0:T(8,128)(2,1)}, bf16[128,1280]{1,0:T(8,128)(2,1)}, u32[]{:S(2)}, u32[]{:S(2)}) collective-permute-start(bf16[128,1280]{1,0:T(8,128)(2,1)} %multiply_convert_fusion.2), channel_id=1, source_target_pairs={{0,1},{1,0},{2,3},{3,2},{4,5},{5,4},{6,7},{7,6},{8,9},{9,8},{10,11... | collective-permute-start | bytes 983048 | tf_op jit(solution)/shard_map/ppermute | solution.py:83
  87.5 8.7 %collective-permute-start.1 = (bf16[128,1280]{1,0:T(8,128)(2,1)}, bf16[128,1280]{1,0:T(8,128)(2,1)}, u32[]{:S(2)}, u32[]{:S(2)}) collective-permute-start(bf16[128,1280]{1,0:T(8,128)(2,1)} %convolution_convert_fusion.1), channel_id=1, source_target_pairs={{0,1},{1,0},{2,3},{3,2},{4,5},{5,4},{6,7},{7,6},{8,9},{9,8},{10,11... | collective-permute-start | bytes 983048 | tf_op jit(solution)/shard_map/ppermute | solution.py:83
  96.2 52.3 %all-to-all-start.2 = ((bf16[64,16,1536]{2,1,0:T(8,128)(2,1)}), bf16[64,16,1536]{2,1,0:T(8,128)(2,1)}, u32[]{:S(2)}, u32[]{:S(2)}) async-start(bf16[64,16,1536]{2,1,0:T(8,128)(2,1)} %bitcast.59), calls=%async_computation.2 | async-start | bytes 6291456 | tf_op jit(solution)/shard_map/all_to_all | solution.py:88
  110.6 3.5 copy-start.9
  114.1 6.8 %copy-start.2 = (f32[128,2048]{1,0:T(8,128)}, f32[128,2048]{1,0:T(8,128)S(1)}, u32[]{:S(2)}) copy-start(f32[128,2048]{1,0:T(8,128)S(1)} %get-tuple-element.41) | copy-start | bytes 3145732
  148.5 79.9 %all-to-all-start.3 = ((bf16[64,16,2560]{2,1,0:T(8,128)(2,1)}), bf16[64,16,2560]{2,1,0:T(8,128)(2,1)}, u32[]{:S(2)}, u32[]{:S(2)}) async-start(bf16[64,16,2560]{2,1,0:T(8,128)(2,1)} %bitcast.57), calls=%async_computation.3 | async-start | bytes 10485760 | tf_op jit(solution)/shard_map/all_to_all | solution.py:88
  253.1 86.0 %copy-start.8 = (s32[64,128]{1,0:T(8,128)S(1)}, s32[64,128]{1,0:T(8,128)}, u32[]{:S(2)}) copy-start(s32[64,128]{1,0:T(8,128)} %copy-done.7) | copy-start | bytes 98308
  253.1 86.5 %copy-start.10 = (s32[1,128,8]{1,2,0:T(8,128)S(1)}, s32[1,128,8]{1,2,0:T(8,128)}, u32[]{:S(2)}) copy-start(s32[1,128,8]{1,2,0:T(8,128)} %param.23) | copy-start | bytes 12292
  253.1 86.5 %copy-start.11 = (f32[1,128,8]{1,2,0:T(8,128)S(1)}, f32[1,128,8]{1,2,0:T(8,128)}, u32[]{:S(2)}) copy-start(f32[1,128,8]{1,2,0:T(8,128)} %param.24) | copy-start | bytes 12292
  253.1 84.3 %all-to-all-start.4 = ((bf16[64,16,2688]{2,1,0:T(8,128)(2,1)}), bf16[64,16,2688]{2,1,0:T(8,128)(2,1)}, u32[]{:S(2)}, u32[]{:S(2)}) async-start(bf16[64,16,2688]{2,1,0:T(8,128)(2,1)} %bitcast.58), calls=%async_computation.4 | async-start | bytes 11010048 | tf_op jit(solution)/shard_map/all_to_all | solution.py:88
  259.9 80.5 %copy-start.4 = (pred[1024,128]{0,1:T(8,128)(4,1)S(1)}, pred[1024,128]{0,1:T(8,128)(4,1)}, u32[]{:S(2)}) copy-start(pred[1024,128]{0,1:T(8,128)(4,1)} %get-tuple-element.27) | copy-start | bytes 393220
  259.9 80.5 %copy-start.5 = (pred[1024,128]{0,1:T(8,128)(4,1)S(1)}, pred[1024,128]{0,1:T(8,128)(4,1)}, u32[]{:S(2)}) copy-start(pred[1024,128]{0,1:T(8,128)(4,1)} %get-tuple-element.33) | copy-start | bytes 393220
  341.6 11.6 %copy-start.1 = (bf16[1280,1280]{1,0:T(8,128)(2,1)S(1)}, bf16[1280,1280]{1,0:T(8,128)(2,1)}, u32[]{:S(2)}) copy-start(bf16[1280,1280]{1,0:T(8,128)(2,1)} %param.20) | copy-start | bytes 9830404

commit v2 on v1

--- a/solution.py
+++ b/solution.py
@@ -21,7 +21,6 @@
 TAIL = CAP - HEAD
 WIDTH = 2048
 PART = WIDTH // 4
-SPLIT = 1024
 HIGHEST = lax.Precision.HIGHEST
 
 
@@ -95,38 +94,40 @@
     return lax.rem(lax.broadcasted_iota(jnp.int32, shape, axis), HEAD) // TAIL
 
 
-def pack_body(split, head_ref, tail_ref, values_ref, *out_refs):
-    head = dot(head_ref[...], values_ref[...]).astype(jnp.bfloat16)
-    quarter = quarter_of((head_ref.shape[0], PART))
+def pack_body(rank_ref, values_ref, out_ref):
+    experts, tokens = rank_ref.shape
+    rows = experts * HEAD
+    rank = jnp.broadcast_to(rank_ref[...][:, None, :], (experts, HEAD, tokens))
+    rank = rank.reshape(rows, tokens)
+    place = lax.rem(lax.broadcasted_iota(jnp.int32, (rows, tokens), 0), HEAD)
+    head = jnp.where(rank == place, 1.0, 0.0).astype(jnp.bfloat16)
+    tail = jnp.where(rank == HEAD + lax.rem(place, TAIL), 1.0, 0.0).astype(jnp.bfloat16)
+    out_ref[:, :WIDTH] = dot(head, values_ref[...]).astype(jnp.bfloat16)
+    quarter = quarter_of((rows, PART))
     packed = jnp.zeros(quarter.shape, jnp.float32)
     for q in range(4):
-        piece = dot(tail_ref[...], values_ref[:, q * PART : (q + 1) * PART])
+        piece = dot(tail, values_ref[:, q * PART : (q + 1) * PART])
         packed = jnp.where(quarter == q, piece, packed)
-    if split:
-        out_refs[0][...] = head[:, :split]
-    out_refs[-1][:, : WIDTH - split] = head[:, split:]
-    out_refs[-1][:, WIDTH - split :] = packed.astype(jnp.bfloat16)
-
-
-def pack(head_picks, tail_picks, values, split=0):
-    rows, tokens = head_picks.shape
-    block = rows // 4
-    widths = ([split] if split else []) + [WIDTH + PART - split]
+    out_ref[:, WIDTH:] = packed.astype(jnp.bfloat16)
+
+
+def pack(rank, values):
+    experts, tokens = rank.shape
+    block = experts // 4
     return pl.pallas_call(
-        functools.partial(pack_body, split),
+        pack_body,
         grid=(4,),
         in_specs=[
             pl.BlockSpec((block, tokens), lambda i: (i, 0)),
-            pl.BlockSpec((block, tokens), lambda i: (i, 0)),
             pl.BlockSpec((tokens, WIDTH), lambda i: (0, 0)),
         ],
-        out_specs=[pl.BlockSpec((block, width), lambda i: (i, 0)) for width in widths],
-        out_shape=[jax.ShapeDtypeStruct((rows, width), jnp.bfloat16) for width in widths],
+        out_specs=pl.BlockSpec((block * HEAD, WIDTH + PART), lambda i: (i, 0)),
+        out_shape=jax.ShapeDtypeStruct((experts * HEAD, WIDTH + PART), jnp.bfloat16),
         cost_estimate=pl.CostEstimate(
-            flops=4 * rows * tokens * WIDTH, bytes_accessed=6_500_000, transcendentals=0
+            flops=4 * experts * HEAD * tokens * WIDTH, bytes_accessed=6_500_000, transcendentals=0
         ),
         name="pack_slots",
-    )(head_picks, tail_picks, values)
+    )(rank, values)
 
 
 def contract_last(left, right):
@@ -146,24 +147,22 @@
         full_ref[head:, q * PART : (q + 1) * PART] = dot(gather, packed).astype(jnp.bfloat16)
 
 
-def back_body(first_ref, second_ref, down_ref, out_ref, full_ref):
-    head = first_ref.shape[0]
-    full_ref[:head, :SPLIT] = first_ref[...]
-    full_ref[:head, SPLIT:] = second_ref[:, : WIDTH - SPLIT]
-    unpack_tail(second_ref[:, WIDTH - SPLIT :], full_ref)
+def back_body(grads_ref, down_ref, out_ref, full_ref):
+    head = grads_ref.shape[0]
+    full_ref[:head, :] = grads_ref[:, :WIDTH]
+    unpack_tail(grads_ref[:, WIDTH:], full_ref)
     out_ref[...] = contract_last(full_ref[...], down_ref[...])
 
 
-def back_run(first, second, down):
-    total = first.shape[0]
+def back_run(grads, down):
+    total = grads.shape[0]
     block = total // 4
     rows = block + block // 4
     return pl.pallas_call(
         back_body,
         grid=(4,),
         in_specs=[
-            pl.BlockSpec((block, first.shape[1]), lambda i: (i, 0)),
-            pl.BlockSpec((block, second.shape[1]), lambda i: (i, 0)),
+            pl.BlockSpec((block, grads.shape[1]), lambda i: (i, 0)),
             pl.BlockSpec(down.shape, lambda i: (0, 0)),
         ],
         out_specs=pl.BlockSpec((rows, down.shape[0]), lambda i: (i, 0)),
@@ -173,7 +172,7 @@
             flops=4_500_000_000, bytes_accessed=13_000_000, transcendentals=0
         ),
         name="back",
-    )(first, second, down)
+    )(grads, down)
 
 
 def expert_body(rows_ref, back_ref, gate_up_ref, out_ref, full_ref):
@@ -299,10 +298,7 @@
     place = jnp.arange(HEAD, dtype=jnp.int32)[None, :, None]
     head_slots = (rank[:, None, :] == place).reshape(-1, tokens)
     tail_slots = (rank[:, None, :] == HEAD + place % TAIL).reshape(-1, tokens)
-    head_picks = head_slots.astype(jnp.bfloat16)
-    tail_picks = tail_slots.astype(jnp.bfloat16)
-    grads_first, grads_second = pack(head_picks, tail_picks, grads, SPLIT)
-    arrived_first = exchange(grads_first)
+    arrived_grads = exchange(pack(rank, grads))
 
     lengths = req_frames[0, 0]
     ends = jnp.cumsum(lengths)
@@ -346,22 +342,18 @@
         hidden = jax.nn.gelu(dot(values, w_up_aud), approximate=False).astype(jnp.bfloat16)
         return dot(hidden, w_down_aud)
 
-    normed_audio, arrived_first = lax.optimization_barrier((normed_audio, arrived_first))
     other = swap(normed_audio)
     theirs = half_product(other).astype(jnp.bfloat16)
     ours = half_product(normed_audio)
     added = swap(theirs)
-    grads_second, added = lax.optimization_barrier((grads_second, added))
-    arrived_second = exchange(grads_second)
     encoded = state + (ours + added.astype(jnp.float32))
     final_audio = layer_norm(encoded).astype(jnp.bfloat16)
     values = dot(final_audio, w_out).astype(jnp.bfloat16).astype(jnp.float32)
     normed = normalize(values, norm_gain).astype(jnp.bfloat16)
 
-    (packed,) = pack(head_picks, tail_picks, normed)
-    packed, arrived_second = lax.optimization_barrier((packed, arrived_second))
-    arrived_rows = exchange(packed)
-    back = back_run(arrived_first, arrived_second, w_down[0])
+    normed, arrived_grads = lax.optimization_barrier((normed, arrived_grads))
+    arrived_rows = exchange(pack(rank, normed))
+    back = back_run(arrived_grads, w_down[0])
     returned = exchange(experts_run(arrived_rows, back, w_gate_up[0]))
 
     weight = jnp.sum(jnp.where(names, gate_weights[0].T[:, None, :], 0.0), axis=0)

time: 355 us -> 339 us (0.955)
  local copies, waits for them, and re-layouts: 14.8 us -> 4.71 us
  other arithmetic: 16.7 us -> 12.3 us
    all_to_all x4 -> x3, waiting for transfers between devices: 190 us -> 142 us  [exchange(): lax.all_to_all(rows.reshape(-1, HEAD, width), ('section', 'ep'), split_ax...]
    ppermute x2, waiting for transfers between devices: 16.8 us -> 64.7 us  [swap(): return lax.ppermute(value, 'dp', [(0, 1), (1, 0)])]
    eq x4, local copies, waits for them, and re-layouts: 4.31 us -> 0.31 us  [shards(): head_slots = (rank[:, None, :] == place).reshape(-1, tokens)]
    convert_element_type x2 -> x0, local copies, waits for them, and re-layouts: 3.61 us -> none  [the longest x1 1.8 us: shards(): head_picks = head_slots.astype(jnp.bfloat16)]
    all_to_all x4 -> x3, starting transfers between devices: 31.4 us -> 30.9 us  [exchange(): lax.all_to_all(rows.reshape(-1, HEAD, width), ('section', 'ep'), split_ax...]
  transfers between devices with their start and end apart: 7 -> 6, of which waited for: 6 -> 4; matrix products, arithmetic and copies ran while one was open for 10% -> 8% of each run, Pallas kernels for 6% -> 4%
where the time goes in v2:
time: 339 us; the launch traced here: 338 us
  waiting for transfers between devices  206 us (61%)
  Pallas kernels  51.6 us (15%)
  starting transfers between devices  40.3 us (12%)
  matrix products  22.1 us (7%)
  other arithmetic  12.3 us (4%)
  local copies, waits for them, and re-layouts  4.71 us (1%)
    all_to_all x3, waiting for transfers between devices, exchange(): lax.all_to_all(rows.reshape(-1, HEAD, width), ('section', 'ep'), split_ax...  142 us
    ppermute x2, waiting for transfers between devices, swap(): return lax.ppermute(value, 'dp', [(0, 1), (1, 0)])  64.7 us
    all_to_all x3, starting transfers between devices, exchange(): lax.all_to_all(rows.reshape(-1, HEAD, width), ('section', 'ep'), split_ax...  30.9 us
    pallas_call x1, Pallas kernels, experts_run(): pl.pallas_call(expert_body, grid=(4,), in_specs=[pl.BlockSpec((block, WID...  24.7 us
    dot_general x5, matrix products, dot(): return jnp.dot(left, right, preferred_element_type=jnp.float32)  17.2 us
    pallas_call x2, Pallas kernels, pack(): pl.pallas_call(pack_body, grid=(4,), in_specs=[pl.BlockSpec((block, token...  10.7 us
    pallas_call x1, Pallas kernels, back_run(): pl.pallas_call(back_body, grid=(4,), in_specs=[pl.BlockSpec((block, grads...  9.22 us
    all_to_all x1, starting transfers between devices, shards(): lax.all_to_all(local_rows.reshape(senders, requests * slab, hop), 'ep', s...  7.83 us
  transfers between devices with their start and end apart: 6, of which 4 were waited for; matrix products, arithmetic and copies ran while one was open for 8% of the time, Pallas kernels for 4%

profile of v2, /device:TPU:11, one launch (start us, length us, event | category | flops | bytes accessed | tf_op | source)
XLA Modules:
  0.0 338.3 jit_solution(16808723005419881536)
XLA Ops:
  0.6 1.2 copy.28
  1.9 0.9 reshape_squeeze.3
  2.8 7.8 %all-to-all-start = ((f32[32,8,160]{2,1,0:T(8,128)}), f32[32,8,160]{2,1,0:T(8,128)S(1)}, u32[]{:S(2)}, u32[]{:S(2)}) async-start(f32[32,8,160]{2,1,0:T(8,128)} %reshape_squeeze.3), calls=%async_computation | async-start | bytes 524288 | tf_op jit(solution)/shard_map/all_to_all | solution.py:284
  11.2 0.8 reduce-window.4
  12.1 0.7 fusion.100
  12.9 1.5 fusion.3.rank_ref
  14.4 5.3 %pack_slots.2 = bf16[1024,2560]{1,0:T(8,128)(2,1)} custom-call(s32[64,128]{1,0:T(8,128)} %fusion.3.rank_ref, bf16[128,2048]{1,0:T(8,128)(2,1)} %bitcast.60), custom_call_target="tpu_custom_call" | custom-call | flops 1073741824 | bytes 6500000 | tf_op jit(solution)/shard_map/pack_slots/pallas_call | solution.py:117
  19.8 11.3 %all-to-all-start.1 = ((bf16[64,16,2560]{2,1,0:T(8,128)(2,1)}), bf16[64,16,2560]{2,1,0:T(8,128)(2,1)}, u32[]{:S(2)}, u32[]{:S(2)}) async-start(bf16[64,16,2560]{2,1,0:T(8,128)(2,1)} %bitcast.55), calls=%async_computation.1 | async-start | bytes 10485760 | tf_op jit(solution)/shard_map/all_to_all | solution.py:87
  32.2 1.9 fusion.101
  34.1 1.2 fusion.2
  35.3 1.2 fusion.185
  38.1 0.8 collective-permute-start
  38.9 55.4 %collective-permute-done = bf16[128,1280]{1,0:T(8,128)(2,1)} collective-permute-done((bf16[128,1280]{1,0:T(8,128)(2,1)S(1)}, bf16[128,1280]{1,0:T(8,128)(2,1)}, u32[]{:S(2)}, u32[]{:S(2)}) %collective-permute-start) | collective-permute-done | bytes 327712 | tf_op jit(solution)/shard_map/ppermute | solution.py:82
  94.3 5.2 %convolution_convert_fusion.1 = bf16[128,1280]{1,0:T(8,128)(2,1)} fusion(bf16[1280,1280]{1,0:T(8,128)(2,1)S(1)} %copy-done, bf16[128,1280]{1,0:T(8,128)(2,1)} %collective-permute-done, bf16[1280,1280]{1,0:T(8,128)(2,1)} %param.19), kind=kOutput, calls=%fused_computation.3 | convolution fusion | flops 849674240 | bytes 7208960 | tf_op jit(solution)/shard_map/dot_general | solution.py:78
  99.5 0.7 collective-permute-start.1
  100.2 9.3 %collective-permute-done.1 = bf16[128,1280]{1,0:T(8,128)(2,1)} collective-permute-done((bf16[128,1280]{1,0:T(8,128)(2,1)}, bf16[128,1280]{1,0:T(8,128)(2,1)}, u32[]{:S(2)}, u32[]{:S(2)}) %collective-permute-start.1) | collective-permute-done | bytes 327712 | tf_op jit(solution)/shard_map/ppermute | solution.py:82
  109.6 5.7 %fusion.180 = (f32[128]{0:T(128)S(1)}, f32[128,1280]{1,0:T(8,128)}) fusion(f32[128,1280]{1,0:T(8,128)} %copy-done.3, bf16[128,1280]{1,0:T(8,128)(2,1)} %collective-permute-done.1, bf16[1280,1280]{1,0:T(8,128)(2,1)S(1)} %copy-done, bf16[1280,1280]{1,0:T(8,128)(2,1)} %param.19, f32[128]{0:T(128)S(1)} %add_rsqrt_fusion.1, f32[128]{0:T(128)S(1)} %broadcast_multiply_fusion.1), kind=kOutput, calls=%fused_computation.260 | convolution fusion | flops 850657152 | bytes 8193536 | tf_op jit(solution)/shard_map/dot_general | solution.py:78
  115.2 1.3 multiply_reduce_fusion.2
  116.5 3.7 %multiply_reduce_fusion.1 = (f32[128]{0:T(128)S(1)}, f32[128,2048]{1,0:T(8,128)S(1)}) fusion(bf16[1280,2048]{1,0:T(8,128)(2,1)} %param.21, f32[128,1280]{1,0:T(8,128)} %get-tuple-element.21, f32[128]{0:T(128)S(1)} %add_rsqrt_fusion, f32[128]{0:T(128)S(1)} %broadcast_multiply_fusion), kind=kOutput, calls=%fused_computation.14 | convolution fusion | flops 672628608 | bytes 6948352 | tf_op jit(solution)/shard_map/dot_general | solution.py:78
  120.3 1.1 multiply_convert_fusion.values_ref
  121.4 5.3 %pack_slots.3 = bf16[1024,2560]{1,0:T(8,128)(2,1)} custom-call(s32[64,128]{1,0:T(8,128)} %fusion.3.rank_ref, bf16[128,2048]{1,0:T(8,128)(2,1)} %multiply_convert_fusion.values_ref), custom_call_target="tpu_custom_call" | custom-call | flops 1073741824 | bytes 6500000 | tf_op jit(solution)/shard_map/pack_slots/pallas_call | solution.py:117
  126.7 12.9 %all-to-all-start.2 = ((bf16[64,16,2560]{2,1,0:T(8,128)(2,1)}), bf16[64,16,2560]{2,1,0:T(8,128)(2,1)}, u32[]{:S(2)}, u32[]{:S(2)}) async-start(bf16[64,16,2560]{2,1,0:T(8,128)(2,1)} %bitcast.56), calls=%async_computation.2 | async-start | bytes 10485760 | tf_op jit(solution)/shard_map/all_to_all | solution.py:87
  139.6 9.2 %back.1.back_ref = f32[1280,768]{1,0:T(8,128)} custom-call(bf16[1024,2560]{1,0:T(8,128)(2,1)} %bitcast.14.grads_ref, bf16[768,2048]{1,0:T(8,128)(2,1)} %bitcast.66), custom_call_target="tpu_custom_call" | custom-call | flops 4499999744 | bytes 13000000 | tf_op jit(solution)/shard_map/back/pallas_call | solution.py:161
  148.8 64.7 %all-to-all-done.2 = bf16[64,16,2560]{2,1,0:T(8,128)(2,1)} async-done(((bf16[64,16,2560]{2,1,0:T(8,128)(2,1)}), bf16[64,16,2560]{2,1,0:T(8,128)(2,1)}, u32[]{:S(2)}, u32[]{:S(2)}) %all-to-all-start.2) | async-done | bytes 5242912 | tf_op jit(solution)/shard_map/all_to_all | solution.py:87
  213.6 24.7 %experts.1 = bf16[1024,2688]{1,0:T(8,128)(2,1)} custom-call(bf16[1024,2560]{1,0:T(8,128)(2,1)} %bitcast.16.rows_ref, f32[1280,768]{1,0:T(8,128)} %back.1.back_ref, bf16[2048,1536]{1,0:T(8,128)(2,1)} %bitcast.65), custom_call_target="tpu_custom_call" | custom-call | flops 16000000000 | bytes 25000000 | tf_op jit(solution)/shard_map/experts/pallas_call | solution.py:216
  238.3 6.8 %all-to-all-start.3 = ((bf16[64,16,2688]{2,1,0:T(8,128)(2,1)}), bf16[64,16,2688]{2,1,0:T(8,128)(2,1)}, u32[]{:S(2)}, u32[]{:S(2)}) async-start(bf16[64,16,2688]{2,1,0:T(8,128)(2,1)} %bitcast.57), calls=%async_computation.3 | async-start | bytes 11010048 | tf_op jit(solution)/shard_map/all_to_all | solution.py:87
  245.6 77.0 %all-to-all-done.3 = bf16[64,16,2688]{2,1,0:T(8,128)(2,1)} async-done(((bf16[64,16,2688]{2,1,0:T(8,128)(2,1)}), bf16[64,16,2688]{2,1,0:T(8,128)(2,1)}, u32[]{:S(2)}, u32[]{:S(2)}) %all-to-all-start.3) | async-done | bytes 5505056 | tf_op jit(solution)/shard_map/all_to_all | solution.py:87
  322.6 1.0 slice_convert_fusion
  325.6 1.1 select_bitcast_fusion
  326.7 7.0 %combine.1 = f32[128,2048]{1,0:T(8,128)} custom-call(f32[128,1024]{1,0:T(8,128)} %get-tuple-element.13.head_ref, f32[128,1024]{1,0:T(8,128)} %get-tuple-element.12.tail_ref, bf16[1024,2688]{1,0:T(8,128)(2,1)} %bitcast.20.rows_ref), custom_call_target="tpu_custom_call" | custom-call | tf_op jit(solution)/shard_map/combine/pallas_call | solution.py:255
  333.7 1.7 multiply_reduce_fusion
  335.5 2.8 fusion.26
  (51 shorter events, 6.0 us)
Async XLA Ops:
  0.6 93.7 %copy-start = (bf16[1280,1280]{1,0:T(8,128)(2,1)S(1)}, bf16[1280,1280]{1,0:T(8,128)(2,1)}, u32[]{:S(2)}) copy-start(bf16[1280,1280]{1,0:T(8,128)(2,1)} %param.20) | copy-start | bytes 9830404
  2.8 17.0 %all-to-all-start = ((f32[32,8,160]{2,1,0:T(8,128)}), f32[32,8,160]{2,1,0:T(8,128)S(1)}, u32[]{:S(2)}, u32[]{:S(2)}) async-start(f32[32,8,160]{2,1,0:T(8,128)} %reshape_squeeze.3), calls=%async_computation | async-start | bytes 524288 | tf_op jit(solution)/shard_map/all_to_all | solution.py:284
  19.8 101.7 %all-to-all-start.1 = ((bf16[64,16,2560]{2,1,0:T(8,128)(2,1)}), bf16[64,16,2560]{2,1,0:T(8,128)(2,1)}, u32[]{:S(2)}, u32[]{:S(2)}) async-start(bf16[64,16,2560]{2,1,0:T(8,128)(2,1)} %bitcast.55), calls=%async_computation.1 | async-start | bytes 10485760 | tf_op jit(solution)/shard_map/all_to_all | solution.py:87
  31.0 5.5 %copy-start.5 = (f32[64,1280]{1,0:T(8,128)S(1)}, f32[64,1280]{1,0:T(8,128)}, u32[]{:S(2)}) copy-start(f32[64,1280]{1,0:T(8,128)} %constant.186.clone) | copy-start | bytes 983044
  37.1 0.9 copy-start.3
  38.1 56.2 %collective-permute-start = (bf16[128,1280]{1,0:T(8,128)(2,1)S(1)}, bf16[128,1280]{1,0:T(8,128)(2,1)}, u32[]{:S(2)}, u32[]{:S(2)}) collective-permute-start(bf16[128,1280]{1,0:T(8,128)(2,1)S(1)} %multiply_convert_fusion.2), channel_id=1, source_target_pairs={{0,1},{1,0},{2,3},{3,2},{4,5},{5,4},{6,7},{7,6},{8,9},{9,8},{10,11... | collective-permute-start | bytes 983048 | tf_op jit(solution)/shard_map/ppermute | solution.py:82
  99.5 10.1 %collective-permute-start.1 = (bf16[128,1280]{1,0:T(8,128)(2,1)}, bf16[128,1280]{1,0:T(8,128)(2,1)}, u32[]{:S(2)}, u32[]{:S(2)}) collective-permute-start(bf16[128,1280]{1,0:T(8,128)(2,1)} %convolution_convert_fusion.1), channel_id=1, source_target_pairs={{0,1},{1,0},{2,3},{3,2},{4,5},{5,4},{6,7},{7,6},{8,9},{9,8},{10,11... | collective-permute-start | bytes 983048 | tf_op jit(solution)/shard_map/ppermute | solution.py:82
  116.5 3.7 %copy-start.6 = (f32[2048]{0:T(1024)S(1)}, f32[2048]{0:T(1024)}, u32[]{:S(2)}) copy-start(f32[2048]{0:T(1024)} %param.22) | copy-start | bytes 24580
  120.2 6.5 %copy-start.2 = (f32[128,2048]{1,0:T(8,128)}, f32[128,2048]{1,0:T(8,128)S(1)}, u32[]{:S(2)}) copy-start(f32[128,2048]{1,0:T(8,128)S(1)} %get-tuple-element.23) | copy-start | bytes 3145732
  126.7 86.8 %all-to-all-start.2 = ((bf16[64,16,2560]{2,1,0:T(8,128)(2,1)}), bf16[64,16,2560]{2,1,0:T(8,128)(2,1)}, u32[]{:S(2)}, u32[]{:S(2)}) async-start(bf16[64,16,2560]{2,1,0:T(8,128)(2,1)} %bitcast.56), calls=%async_computation.2 | async-start | bytes 10485760 | tf_op jit(solution)/shard_map/all_to_all | solution.py:87
  238.3 7.0 %copy-start.4 = (s32[64,128]{1,0:T(8,128)S(1)}, s32[64,128]{1,0:T(8,128)}, u32[]{:S(2)}) copy-start(s32[64,128]{1,0:T(8,128)} %fusion.3.rank_ref) | copy-start | bytes 98308
  238.3 84.3 %all-to-all-start.3 = ((bf16[64,16,2688]{2,1,0:T(8,128)(2,1)}), bf16[64,16,2688]{2,1,0:T(8,128)(2,1)}, u32[]{:S(2)}, u32[]{:S(2)}) async-start(bf16[64,16,2688]{2,1,0:T(8,128)(2,1)} %bitcast.57), calls=%async_computation.3 | async-start | bytes 11010048 | tf_op jit(solution)/shard_map/all_to_all | solution.py:87
  245.1 79.6 %copy-start.7 = (s32[1,128,8]{1,2,0:T(8,128)S(1)}, s32[1,128,8]{1,2,0:T(8,128)}, u32[]{:S(2)}) copy-start(s32[1,128,8]{1,2,0:T(8,128)} %param.23) | copy-start | bytes 12292
  245.1 79.6 %copy-start.8 = (f32[1,128,8]{1,2,0:T(8,128)S(1)}, f32[1,128,8]{1,2,0:T(8,128)}, u32[]{:S(2)}) copy-start(f32[1,128,8]{1,2,0:T(8,128)} %param.24) | copy-start | bytes 12292
  326.7 11.6 %copy-start.1 = (bf16[1280,1280]{1,0:T(8,128)(2,1)S(1)}, bf16[1280,1280]{1,0:T(8,128)(2,1)}, u32[]{:S(2)}) copy-start(bf16[1280,1280]{1,0:T(8,128)(2,1)} %param.20) | copy-start | bytes 9830404
